TPU v7x, 32 devices: a whole 2x2x4 slice. The times are simulated.
32 devices in a mesh: dp: 8 (over z, x), tp: 4 (over y, core).
Axes of the slice: x: 2, y: 2, z: 4, core: 2. Of those that a mesh axis runs over, the one named last changes fastest.
Arguments:
- inputs: bfloat16 [2, 4096, 768], P(None, 'dp'), may hold values from -6 to 6
- cotangent: bfloat16 [2, 4096, 768], P(None, 'dp'), may hold values from -6 to 6
- item_ids: int32 [2, 4096], P(None, 'dp'), may hold values from 0 to 3584, as said below
- timestep: int32 [2, 8], P(None, 'dp'), may hold values from 0 to 999
- qkv_weight: float32 [768, 3, 768], P('dp', None, 'tp'), may hold values from -0.21875 to 0.21875
- out_weight: float32 [768, 768], P('tp', 'dp'), may hold values from -0.625 to 0.625
- up_weight: float32 [768, 3072], P('dp', 'tp'), may hold values from -0.21875 to 0.21875
- down_weight: float32 [3072, 768], P('tp', 'dp'), may hold values from -0.109375 to 0.109375
- norm_params: float32 [4, 768], P(None, 'dp')
- qkv_first: float32 [768, 3, 768], P('dp', None, 'tp'), may hold values from -0.00061035156 to 0.00061035156
- out_first: float32 [768, 768], P('tp', 'dp'), may hold values from -0.00061035156 to 0.00061035156
- up_first: float32 [768, 3072], P('dp', 'tp'), may hold values from -0.00061035156 to 0.00061035156
- down_first: float32 [3072, 768], P('tp', 'dp'), may hold values from -0.00061035156 to 0.00061035156
- norm_first: float32 [4, 768], P(None, 'dp'), may hold values from -0.001953125 to 0.001953125
- qkv_second: float32 [768, 3, 768], P('dp', None, 'tp'), may hold values from 1.4122378e-10 to 5.6489513e-10
- out_second: float32 [768, 768], P('tp', 'dp'), may hold values from 1.4122378e-10 to 5.6489513e-10
- up_second: float32 [768, 3072], P('dp', 'tp'), may hold values from 1.4122378e-10 to 5.6489513e-10
- down_second: float32 [3072, 768], P('tp', 'dp'), may hold values from 1.4122378e-10 to 5.6489513e-10
- norm_second: float32 [4, 768], P(None, 'dp'), may hold values from 1.4122379e-09 to 5.6489515e-09
Outputs:
- block_out: bfloat16 [2, 4096, 768], P(None, 'dp')
- input_grad: float32 [2, 4096, 768], P(None, 'dp')
- grad_norm: float32 [], replicated
- qkv_new: float32 [768, 3, 768], P('dp', None, 'tp')
- qkv_first_new: float32 [768, 3, 768], P('dp', None, 'tp')
- qkv_second_new: float32 [768, 3, 768], P('dp', None, 'tp')
- out_new: float32 [768, 768], P('tp', 'dp')
- out_first_new: float32 [768, 768], P('tp', 'dp')
- out_second_new: float32 [768, 768], P('tp', 'dp')
- up_new: float32 [768, 3072], P('dp', 'tp')
- up_first_new: float32 [768, 3072], P('dp', 'tp')
- up_second_new: float32 [768, 3072], P('dp', 'tp')
- down_new: float32 [3072, 768], P('tp', 'dp')
- down_first_new: float32 [3072, 768], P('tp', 'dp')
- down_second_new: float32 [3072, 768], P('tp', 'dp')
- norm_new: float32 [4, 768], P(None, 'dp')
- norm_first_new: float32 [4, 768], P(None, 'dp')
- norm_second_new: float32 [4, 768], P(None, 'dp')
Inputs may be any that keep to these rules, and one draw needn't show every extreme that they name: `item_ids`: A token's id is the index, within its micro-batch, of its item's first token, so ids never decrease along a micro-batch; every block of 512 tokens of one index of dp starts a new item, so no item spans two blocks; an item has 1 to 512 tokens and in every draw some item has exactly 512.
All inputs are finite; a program needn't handle non-finite values.
Results may differ from a plain program's by a relative error of at most 0.009.
Values may be sent and summed in bfloat16 or wider, within the bound.
A program may use at most 128 MiB of HBM per device.

v0:
```python
from functools import partial
import math
import jax
import jax.numpy as jnp
from jax import lax
from jax.sharding import PartitionSpec as P

HEAD_DIM = 64
STEP = 10
norm_eps = 1e-05
clip_limit = 1.0
learn_rate = 0.02
beta_one = 0.9
beta_two = 0.999
adam_eps = 1e-08
weight_decay = 0.01


def time_embed(step_values, model_width):
    half_width = model_width // 2
    frequency = jnp.exp(
        jnp.arange(half_width, dtype=jnp.float32) * (-math.log(10000.0) / half_width)
    )
    angles = step_values.astype(jnp.float32)[..., None] * frequency
    return jnp.concatenate([jnp.sin(angles), jnp.cos(angles)], axis=-1)


def layer_norm(values, gain_row, bias_row):
    centre = values - jnp.mean(values, axis=-1, keepdims=True)
    spread = jnp.mean(centre * centre, axis=-1, keepdims=True)
    return centre * lax.rsqrt(spread + norm_eps) * gain_row + bias_row


def masked_scores(query_rows, key_rows, same_item, score_scale):
    scores = (
        jnp.einsum("thd,shd->hts", query_rows, key_rows, preferred_element_type=jnp.float32)
        * score_scale
    )
    return jnp.where(same_item, scores, -1e30)


def one_micro(gathered, stream_in, upstream, labels, embed_row):
    qkv_mat, out_mat, up_mat, down_mat, norm_rows = gathered
    tokens_here = stream_in.shape[0]
    local_width = out_mat.shape[0]
    heads_here = local_width // HEAD_DIM
    score_scale = 1.0 / math.sqrt(HEAD_DIM)
    split_shape = (tokens_here, heads_here, HEAD_DIM)
    norm_gains = norm_rows.astype(jnp.float32)
    gain_one = 1.0 + norm_gains[0]
    gain_two = 1.0 + norm_gains[2]
    stream = stream_in.astype(jnp.float32) + embed_row[None, :]
    normed_f, norm_one_back = jax.vjp(layer_norm, stream, gain_one, norm_gains[1])
    normed = normed_f.astype(jnp.bfloat16)
    triple = jnp.einsum("td,dje->jte", normed, qkv_mat, preferred_element_type=jnp.float32).astype(
        jnp.bfloat16
    )
    query_rows = triple[0].reshape(split_shape)
    key_rows = triple[1].reshape(split_shape)
    value_rows = triple[2].reshape(split_shape)
    same_item = (labels[:, None] == labels[None, :])[None]
    scores = masked_scores(query_rows, key_rows, same_item, score_scale)
    row_top = jnp.max(scores, axis=-1, keepdims=True)
    exp_scores = jnp.exp(scores - row_top)
    row_total = jnp.sum(exp_scores, axis=-1, keepdims=True)
    probs_soft = exp_scores / row_total
    log_total = row_top + jnp.log(row_total)
    context = (
        jnp.einsum(
            "hts,shd->thd",
            probs_soft.astype(jnp.bfloat16),
            value_rows,
            preferred_element_type=jnp.float32,
        )
        .reshape(tokens_here, local_width)
        .astype(jnp.bfloat16)
    )
    attn_out = lax.psum(jnp.dot(context, out_mat, preferred_element_type=jnp.float32), "tp")
    middle = stream + attn_out
    normed_two_f, norm_two_back = jax.vjp(layer_norm, middle, gain_two, norm_gains[3])
    normed_two = normed_two_f.astype(jnp.bfloat16)
    hidden_pre = jnp.dot(normed_two, up_mat, preferred_element_type=jnp.float32)
    hidden_f, gelu_back = jax.vjp(partial(jax.nn.gelu, approximate=False), hidden_pre)
    hidden = hidden_f.astype(jnp.bfloat16)
    branch = lax.psum(
        jnp.dot(hidden, down_mat, preferred_element_type=jnp.float32).astype(jnp.bfloat16), "tp"
    ).astype(jnp.float32)
    block_out = (middle + branch).astype(jnp.bfloat16)
    grad_down = jnp.einsum("tf,td->fd", hidden, upstream, preferred_element_type=jnp.float32)
    grad_hidden = jnp.einsum("td,fd->tf", upstream, down_mat, preferred_element_type=jnp.float32)
    grad_pre = gelu_back(grad_hidden)[0].astype(jnp.bfloat16)
    grad_up = jnp.einsum("td,tf->df", normed_two, grad_pre, preferred_element_type=jnp.float32)
    grad_normed_two = lax.psum(
        jnp.einsum("tf,df->td", grad_pre, up_mat, preferred_element_type=jnp.float32), "tp"
    )
    grad_middle_norm, grad_gain_two, grad_bias_two = norm_two_back(grad_normed_two)
    grad_middle = upstream.astype(jnp.float32) + grad_middle_norm
    grad_attn = grad_middle.astype(jnp.bfloat16)
    grad_outmat = jnp.einsum("tc,td->cd", context, grad_attn, preferred_element_type=jnp.float32)
    grad_context = (
        jnp.einsum("td,cd->tc", grad_attn, out_mat, preferred_element_type=jnp.float32)
        .astype(jnp.bfloat16)
        .reshape(split_shape)
    )
    probs_again = jnp.exp(masked_scores(query_rows, key_rows, same_item, score_scale) - log_total)
    grad_values = jnp.einsum(
        "hts,thd->shd",
        probs_again.astype(jnp.bfloat16),
        grad_context,
        preferred_element_type=jnp.float32,
    )
    grad_probs = jnp.einsum(
        "thd,shd->hts", grad_context, value_rows, preferred_element_type=jnp.float32
    )
    inner_sum = jnp.sum(grad_probs * probs_again, axis=-1, keepdims=True)
    grad_scores = (probs_again * (grad_probs - inner_sum)).astype(jnp.bfloat16)
    grad_query = (
        jnp.einsum("hts,shd->thd", grad_scores, key_rows, preferred_element_type=jnp.float32)
        * score_scale
    )
    grad_key = (
        jnp.einsum("hts,thd->shd", grad_scores, query_rows, preferred_element_type=jnp.float32)
        * score_scale
    )
    grad_triple = (
        jnp.stack([grad_query, grad_key, grad_values])
        .reshape(3, tokens_here, local_width)
        .astype(jnp.bfloat16)
    )
    grad_qkv = jnp.einsum("td,jte->dje", normed, grad_triple, preferred_element_type=jnp.float32)
    grad_normed = lax.psum(
        jnp.einsum("jte,dje->td", grad_triple, qkv_mat, preferred_element_type=jnp.float32).astype(
            jnp.bfloat16
        ),
        "tp",
    ).astype(jnp.float32)
    grad_stream_norm, grad_gain_one, grad_bias_one = norm_one_back(grad_normed)
    grad_input = grad_middle + grad_stream_norm
    grad_norms = jnp.stack([grad_gain_one, grad_bias_one, grad_gain_two, grad_bias_two])
    return (block_out, grad_input, (grad_qkv, grad_outmat, grad_up, grad_down, grad_norms))


def adam_step(weight, gradient, first_old, second_old):
    first_new = beta_one * first_old + (1.0 - beta_one) * gradient
    second_new = beta_two * second_old + (1.0 - beta_two) * gradient * gradient
    moment_one = first_new / (1.0 - beta_one**STEP)
    moment_two = second_new / (1.0 - beta_two**STEP)
    weight_new = weight - learn_rate * (
        moment_one / (jnp.sqrt(moment_two) + adam_eps) + weight_decay * weight
    )
    return (weight_new, first_new, second_new)


def local(
    inputs,
    cotangent,
    item_ids,
    timestep,
    qkv_weight,
    out_weight,
    up_weight,
    down_weight,
    norm_params,
    qkv_first,
    out_first,
    up_first,
    down_first,
    norm_first,
    qkv_second,
    out_second,
    up_second,
    down_second,
    norm_second,
):
    micro_count = inputs.shape[0]
    embeds = time_embed(timestep[:, 0], inputs.shape[2])
    qkv_low = qkv_weight.astype(jnp.bfloat16)
    out_low = out_weight.astype(jnp.bfloat16)
    up_low = up_weight.astype(jnp.bfloat16)
    down_low = down_weight.astype(jnp.bfloat16)
    norm_low = norm_params.astype(jnp.bfloat16)
    block_list = []
    input_list = []
    for number in range(micro_count):
        gathered = (
            lax.all_gather(qkv_low, "dp", axis=0, tiled=True),
            lax.all_gather(out_low, "dp", axis=1, tiled=True),
            lax.all_gather(up_low, "dp", axis=0, tiled=True),
            lax.all_gather(down_low, "dp", axis=1, tiled=True),
            lax.all_gather(norm_low, "dp", axis=1, tiled=True),
        )
        block_out, grad_input, grad_list = one_micro(
            gathered, inputs[number], cotangent[number], item_ids[number], embeds[number]
        )
        owned_grads = (
            lax.psum_scatter(grad_list[0], "dp", scatter_dimension=0, tiled=True),
            lax.psum_scatter(grad_list[1], "dp", scatter_dimension=1, tiled=True),
            lax.psum_scatter(grad_list[2], "dp", scatter_dimension=0, tiled=True),
            lax.psum_scatter(grad_list[3], "dp", scatter_dimension=1, tiled=True),
            lax.psum_scatter(grad_list[4], "dp", scatter_dimension=1, tiled=True),
        )
        if number == 0:
            totals = tuple(owned_grads)
        else:
            totals = tuple((left + right for left, right in zip(totals, owned_grads)))
        block_list.append(block_out)
        input_list.append(grad_input)
    own_squares = jnp.sum(totals[0] * totals[0]) + jnp.sum(totals[1] * totals[1])
    own_squares = own_squares + jnp.sum(totals[2] * totals[2]) + jnp.sum(totals[3] * totals[3])
    norm_squares = jnp.sum(totals[4] * totals[4])
    own_squares = own_squares + jnp.where(
        lax.axis_index("tp") == 0, norm_squares, jnp.zeros_like(norm_squares)
    )
    grad_norm = jnp.sqrt(lax.psum(own_squares, ("dp", "tp")))
    factor = jnp.minimum(1.0, clip_limit / (grad_norm + 1e-06))
    weights = (qkv_weight, out_weight, up_weight, down_weight, norm_params)
    firsts = (qkv_first, out_first, up_first, down_first, norm_first)
    seconds = (qkv_second, out_second, up_second, down_second, norm_second)
    result = [
        adam_step(weights[index], totals[index] * factor, firsts[index], seconds[index])
        for index in range(5)
    ]
    return (
        jnp.stack(block_list),
        jnp.stack(input_list),
        grad_norm,
        result[0][0],
        result[0][1],
        result[0][2],
        result[1][0],
        result[1][1],
        result[1][2],
        result[2][0],
        result[2][1],
        result[2][2],
        result[3][0],
        result[3][1],
        result[3][2],
        result[4][0],
        result[4][1],
        result[4][2],
    )


def solution(mesh):
    return jax.shard_map(
        local,
        mesh=mesh,
        in_specs=(
            P(None, "dp", None),
            P(None, "dp", None),
            P(None, "dp"),
            P(None, "dp"),
            P("dp", None, "tp"),
            P("tp", "dp"),
            P("dp", "tp"),
            P("tp", "dp"),
            P(None, "dp"),
            P("dp", None, "tp"),
            P("tp", "dp"),
            P("dp", "tp"),
            P("tp", "dp"),
            P(None, "dp"),
            P("dp", None, "tp"),
            P("tp", "dp"),
            P("dp", "tp"),
            P("tp", "dp"),
            P(None, "dp"),
        ),
        out_specs=(
            P(None, "dp", None),
            P(None, "dp", None),
            P(),
            P("dp", None, "tp"),
            P("dp", None, "tp"),
            P("dp", None, "tp"),
            P("tp", "dp"),
            P("tp", "dp"),
            P("tp", "dp"),
            P("dp", "tp"),
            P("dp", "tp"),
            P("dp", "tp"),
            P("tp", "dp"),
            P("tp", "dp"),
            P("tp", "dp"),
            P(None, "dp"),
            P(None, "dp"),
            P(None, "dp"),
        ),
        check_vma=False,
    )
```

profile of v0, /device:TPU:0, one launch (start us, length us, event | category | flops | bytes accessed | tf_op | source)
XLA Modules:
  0.0 723.9 jit_solution(8021237277195858394)
XLA Ops:
  12.2 22.2 %all-gather = bf16[8,96,4]{1,2,0:T(4,128)(2,1)S(1)} all-gather(bf16[1,96,4]{1,2,0:T(4,128)(2,1)S(1)} %convert_bitcast_fusion.2), channel_id=1, replica_groups=mesh['dp'=8,'tp'=4] {'dp'}, dimensions={0}, use_global_device_ids=true | all-gather | bytes 6912 | tf_op jit(solution)/shard_map/all_gather | solution.py:190
  35.3 35.3 %all_gather.21 = bf16[768,3,192]{2,1,0:T(4,128)(2,1)S(1)} all-gather(bf16[96,3,192]{2,1,0:T(4,128)(2,1)S(1)} %copy.82), channel_id=1, replica_groups=mesh['dp'=8,'tp'=4] {'dp'}, dimensions={0}, use_global_device_ids=true | all-gather | bytes 995328 | tf_op jit(solution)/shard_map/all_gather | solution.py:186
  77.2 31.1 %all_gather.22 = bf16[192,768]{0,1:T(8,128)(2,1)S(1)} all-gather(bf16[192,96]{0,1:T(8,128)(2,1)S(1)} %copy.85), channel_id=1, replica_groups=mesh['dp'=8,'tp'=4] {'dp'}, dimensions={1}, use_global_device_ids=true | all-gather | bytes 331776 | tf_op jit(solution)/shard_map/all_gather | solution.py:187
  124.4 64.3 %all-reduce.9.cloned.1.call-done = (f32[512,768]{1,0:T(8,128)}, f32[512,768]{1,0:T(8,128)}) async-done(((f32[512,768]{1,0:T(8,128)}, f32[512,768]{1,0:T(8,128)}), (f32[512,768]{1,0:T(8,128)}, f32[512,768]{1,0:T(8,128)})) %all-reduce.9.cloned.1.call-update) | async-done | bytes 3145744 | tf_op jit(solution)/shard_map/psum | solution.py:78
  188.7 3.0 fusion.123
  194.6 7.6 %multiply_convert_fusion.3 = (bf16[512,768]{1,0:T(8,128)(2,1)}, f32[512,768]{1,0:T(8,128)}, f32[512,768]{1,0:T(8,128)}) fusion(bf16[768,768]{1,0:T(8,128)(2,1)} %all-gather.4.cloned.1.call-done, f32[512,768]{1,0:T(8,128)} %copy-done.8, f32[768]{0:T(1024)} %get-tuple-element.39, f32[768]{0:T(1024)} %get-tuple-element.38, f32[512]{0:T(512)} %fusion.99, ...), kind=kOutput, calls=%fused_computation.98 | convolution fusion | flops 631504896 | bytes 6694912 | tf_op jit(solution)/shard_map/dot_general | solution.py:82
  202.2 4.3 all-gather.6.cloned.1.call-done
  206.5 3.6 add_convert_fusion.1
  213.1 5.0 multiply_convert_fusion.2
  224.3 3.4 convolution_convert_fusion.1
  229.5 59.9 %all-reduce.7.cloned.1.call-done = (f32[512,768]{1,0:T(8,128)}, f32[512,768]{1,0:T(8,128)}) async-done(((f32[512,768]{1,0:T(8,128)}, f32[512,768]{1,0:T(8,128)}), (f32[512,768]{1,0:T(8,128)}, f32[512,768]{1,0:T(8,128)})) %all-reduce.7.cloned.1.call-update) | async-done | bytes 3145744 | tf_op jit(solution)/shard_map/psum | solution.py:93
  289.4 4.7 multiply_reduce_fusion.3
  312.8 3.5 fusion.112
  319.4 61.3 %all-reduce.11.cloned.1.call-done = (bf16[512,768]{1,0:T(8,128)(2,1)}, bf16[512,768]{1,0:T(8,128)(2,1)}, bf16[512,768]{1,0:T(8,128)(2,1)}, bf16[512,768]{1,0:T(8,128)(2,1)}) async-done(((bf16[512,768]{1,0:T(8,128)(2,1)}, bf16[512,768]{1,0:T(8,128)(2,1)}, bf16[512,768]{1,0:T(8,128)(2,1)}, bf16[512,768]{1,0:T(8,128)(2,1)}), (bf16[512,768]{1,0:T(8,128)(2,1)}, bf16[512,768]{1,0:T(8,128)(2,1)}, ...) | async-done | bytes 3145744 | tf_op jit(solution)/shard_map/psum | solution.py:85
  380.8 2.5 fusion.9
  383.5 2.5 fusion.12
  387.2 4.4 convolution_add_fusion.1
  399.5 2.5 convolution_add_fusion.2
  403.8 2.8 add_bitcast_fusion.1
  411.7 37.1 %reduce-scatter.18.cloned.1.call-done = f32[96,4]{1,0:T(8,128)} async-done(((f32[768,4]{1,0:T(8,128)}), f32[96,4]{1,0:T(8,128)}) %reduce-scatter.18.cloned.1.call-update) | async-done | bytes 1552
  450.9 70.0 %reduce-scatter.12.cloned.1.call-done = f32[96,768]{1,0:T(8,128)} async-done(((f32[768,768]{1,0:T(8,128)}), f32[96,768]{1,0:T(8,128)}) %reduce-scatter.12.cloned.1.call-update) | async-done | bytes 294928 | tf_op jit(solution)/shard_map/reduce_scatter | solution.py:198
  522.6 70.3 %reduce-scatter.14.cloned.1.call-done = f32[768,96]{0,1:T(8,128)} async-done(((f32[768,768]{0,1:T(8,128)}), f32[768,96]{0,1:T(8,128)}) %reduce-scatter.14.cloned.1.call-update) | async-done | bytes 294928 | tf_op jit(solution)/shard_map/reduce_scatter | solution.py:199
  594.6 70.2 %reduce-scatter.10.cloned.1.call-done = f32[96,3,192]{2,0,1:T(8,128)} async-done(((f32[768,3,192]{2,0,1:T(8,128)}), f32[96,3,192]{2,0,1:T(8,128)}) %reduce-scatter.10.cloned.1.call-update) | async-done | bytes 221200 | tf_op jit(solution)/shard_map/reduce_scatter | solution.py:196
  670.4 39.6 %psum.71 = f32[]{:T(128)} all-reduce(f32[]{:T(128)S(6)} %add.323), channel_id=1, replica_groups=mesh['dp'=8,'tp'=4] {'dp','tp'}, use_global_device_ids=true, to_apply=%region_53.54 | all-reduce | flops 1 | bytes 8 | tf_op jit(solution)/shard_map/psum | solution.py:214
  (417 shorter events, 90.2 us)
Async XLA Ops:
  8.0 180.7 %all-reduce.9.cloned.1.call-start = ((), (), s32[]{:S(2)}) async-start(), calls=%async_computation.13 | async-start | bytes 6291456 | tf_op jit(solution)/shard_map/psum | solution.py:78
  10.8 61.8 %copy-start.85 = (f32[512]{0:T(512)}, f32[512]{0:T(512)S(1)}, u32[]{:S(2)}) copy-start(f32[512]{0:T(512)S(1)} %get-tuple-element.109) | copy-start | bytes 6148
  10.9 97.4 %copy-start.83 = (f32[512]{0:T(512)}, f32[512]{0:T(512)S(1)}, u32[]{:S(2)}) copy-start(f32[512]{0:T(512)S(1)} %get-tuple-element.108) | copy-start | bytes 6148
  12.1 60.5 %copy-start.104 = (f32[512]{0:T(512)}, f32[512]{0:T(512)S(1)}, u32[]{:S(2)}) copy-start(f32[512]{0:T(512)S(1)} %fusion.98) | copy-start | bytes 6148
  35.1 73.2 %copy-start.75 = (f32[768]{0:T(1024)}, f32[768]{0:T(1024)S(1)}, u32[]{:S(2)}) copy-start(f32[768]{0:T(1024)S(1)} %get-tuple-element.41) | copy-start | bytes 9220
  120.4 74.2 %all-gather.4.cloned.1.call-start = ((), (), s32[]{:S(2)}) async-start(), calls=%async_computation.5 | async-start | bytes 1327104 | tf_op jit(solution)/shard_map/all_gather | solution.py:188
  122.1 84.4 %all-gather.6.cloned.1.call-start = ((), (), s32[]{:S(2)}) async-start(), calls=%async_computation.6 | async-start | bytes 1327104 | tf_op jit(solution)/shard_map/all_gather | solution.py:189
  123.8 165.6 %all-reduce.7.cloned.1.call-start = ((), (), s32[]{:S(2)}) async-start(), calls=%async_computation.12 | async-start | bytes 6291456 | tf_op jit(solution)/shard_map/psum | solution.py:93
  222.1 158.7 %all-reduce.11.cloned.1.call-start = ((), (), s32[]{:S(2)}) async-start(), calls=%async_computation.14 | async-start | bytes 6291456 | tf_op jit(solution)/shard_map/psum | solution.py:85
  311.5 90.5 %reduce-scatter.16.cloned.1.call-start = ((), (), s32[]{:S(2)}) async-start(), calls=%async_computation.10 | async-start | bytes 884736
  318.1 62.6 %copy-start.3 = (bf16[2,512,768]{2,1,0:T(8,128)(2,1)S(1)}, bf16[2,512,768]{2,1,0:T(8,128)(2,1)}, u32[]{:S(2)}) copy-start(bf16[2,512,768]{2,1,0:T(8,128)(2,1)} %param.19) | copy-start | bytes 4718596
  318.1 62.6 %copy-start.76 = (f32[768]{0:T(1024)S(1)}, f32[768]{0:T(1024)}, u32[]{:S(2)}) copy-start(f32[768]{0:T(1024)} %copy-done.75) | copy-start | bytes 9220
  318.2 62.6 %copy-start.84 = (f32[512]{0:T(512)S(1)}, f32[512]{0:T(512)}, u32[]{:S(2)}) copy-start(f32[512]{0:T(512)} %copy-done.83) | copy-start | bytes 6148
  318.2 62.6 %copy-start.86 = (f32[512]{0:T(512)S(1)}, f32[512]{0:T(512)}, u32[]{:S(2)}) copy-start(f32[512]{0:T(512)} %copy-done.85) | copy-start | bytes 6148
  319.4 129.4 %reduce-scatter.18.cloned.1.call-start = ((), (), s32[]{:S(2)}) async-start(), calls=%async_computation.11 | async-start | bytes 442368
  387.1 133.9 %reduce-scatter.12.cloned.1.call-start = ((), (), s32[]{:S(2)}) async-start(), calls=%async_computation.8 | async-start | bytes 2654208 | tf_op jit(solution)/shard_map/reduce_scatter | solution.py:198
  391.6 201.4 %reduce-scatter.14.cloned.1.call-start = ((), (), s32[]{:S(2)}) async-start(), calls=%async_computation.9 | async-start | bytes 2654208 | tf_op jit(solution)/shard_map/reduce_scatter | solution.py:199
  396.3 268.4 %reduce-scatter.10.cloned.1.call-start = ((), (), s32[]{:S(2)}) async-start(), calls=%async_computation.7 | async-start | bytes 2654208 | tf_op jit(solution)/shard_map/reduce_scatter | solution.py:196
  669.1 43.0 %copy-start.36 = (f32[768,96]{0,1:T(8,128)S(1)}, f32[768,96]{0,1:T(8,128)}, u32[]{:S(2)}) copy-start(f32[768,96]{0,1:T(8,128)} %param.26) | copy-start | bytes 884740
  669.1 43.0 %copy-start.41 = (f32[768,96]{0,1:T(8,128)S(1)}, f32[768,96]{0,1:T(8,128)}, u32[]{:S(2)}) copy-start(f32[768,96]{0,1:T(8,128)} %reduce-scatter.14.cloned.1.call-done) | copy-start | bytes 884740
  669.1 43.0 %copy-start.60 = (f32[768,96]{0,1:T(8,128)S(1)}, f32[768,96]{0,1:T(8,128)}, u32[]{:S(2)}) copy-start(f32[768,96]{0,1:T(8,128)} %param.31) | copy-start | bytes 884740
  669.1 43.0 %copy-start.61 = (f32[768,96]{0,1:T(8,128)S(1)}, f32[768,96]{0,1:T(8,128)}, u32[]{:S(2)}) copy-start(f32[768,96]{0,1:T(8,128)} %param.36) | copy-start | bytes 884740
  670.4 42.8 %copy-start.62 = (f32[96,768]{1,0:T(8,128)S(1)}, f32[96,768]{1,0:T(8,128)}, u32[]{:S(2)}) copy-start(f32[96,768]{1,0:T(8,128)} %param.30) | copy-start | bytes 884740
  670.4 42.8 %copy-start.63 = (f32[96,768]{1,0:T(8,128)S(1)}, f32[96,768]{1,0:T(8,128)}, u32[]{:S(2)}) copy-start(f32[96,768]{1,0:T(8,128)} %param.35) | copy-start | bytes 884740
  (131 other events, 842.6 us)
Sparse Core Ops, SparseCore 0:
  120.5 68.1 all-reduce.8
  222.2 67.1 all-reduce.6
  311.6 69.1 all-reduce.10
Sparse Core Ops, SparseCore 1:
  123.6 40.9 all-gather.3
  166.6 39.9 all-gather.5
  319.5 62.4 reduce-scatter.15
  387.2 61.6 reduce-scatter.17
  452.7 68.2 reduce-scatter.11
  524.9 68.0 reduce-scatter.13
  596.7 68.0 reduce-scatter.9
where the time goes:
time: 731 us; the launch traced here: 724 us
  waiting for transfers between devices  438 us (60%)
  blocking collectives  128 us (18%)
  matrix products  63.2 us (9%)
  other arithmetic  47.9 us (7%)
  local copies, waits for them, and re-layouts  22.8 us (3%)
  between operations  22.4 us (3%)
    reduce_scatter x1, waiting for transfers between devices, local(): lax.psum_scatter(grad_list[3], 'dp', scatter_dimension=1, tiled=True)  70.3 us
    reduce_scatter x1, waiting for transfers between devices, local(): lax.psum_scatter(grad_list[0], 'dp', scatter_dimension=0, tiled=True)  70.2 us
    reduce_scatter x1, waiting for transfers between devices, local(): lax.psum_scatter(grad_list[2], 'dp', scatter_dimension=0, tiled=True)  70 us
    psum x1, waiting for transfers between devices, one_micro(): lax.psum(jnp.dot(context, out_mat, preferred_element_type=jnp.float32), '...  64.3 us
    psum x1, waiting for transfers between devices, one_micro(): lax.psum(jnp.dot(hidden, down_mat, preferred_element_type=jnp.float32).as...  61.3 us
    psum x1, waiting for transfers between devices, one_micro(): lax.psum(jnp.einsum('tf,df->td', grad_pre, up_mat, preferred_element_type...  59.9 us
    psum x1, blocking collectives, local(): grad_norm = jnp.sqrt(lax.psum(own_squares, ('dp', 'tp')))  39.6 us
    unnamed x12, waiting for transfers between devices  37.3 us
  transfers between devices with their start and end apart: 10, of which 8 were waited for; matrix products, arithmetic and copies ran while one was open for 8% of the time, Pallas kernels for 0%

commit v1 on v0

--- a/solution.py
+++ b/solution.py
@@ -1,3 +1,4 @@
+import functools
 from functools import partial
 import math
 import jax
@@ -14,6 +15,31 @@
 beta_two = 0.999
 adam_eps = 1e-08
 weight_decay = 0.01
+
+
+def pair_values(block_here, comm_axis, at_axis):
+    known, side_arr, field_out = (
+        lax.axis_size(comm_axis),
+        lax.axis_index(comm_axis),
+        block_here.shape[at_axis],
+    )
+    queue = tuple(((q, (q + 1) % known) for q in range(known)))
+    current_value = jnp.zeros(
+        (*block_here.shape[:at_axis], known * field_out, *block_here.shape[at_axis + 1 :]),
+        block_here.dtype,
+    )
+    local_out = block_here
+    for src_i in range(known):
+        z_new = (side_arr - src_i) % known
+        current_value = lax.dynamic_update_slice_in_dim(
+            current_value, local_out, z_new * field_out, axis=at_axis
+        )
+        if src_i < known - 1:
+            local_out = lax.ppermute(local_out, axis_name=comm_axis, perm=queue)
+    return current_value
+
+
+zone_choose = functools.partial(pair_values, comm_axis="dp", at_axis=1)
 
 
 def time_embed(step_values, model_width):
@@ -184,7 +210,7 @@
     for number in range(micro_count):
         gathered = (
             lax.all_gather(qkv_low, "dp", axis=0, tiled=True),
-            lax.all_gather(out_low, "dp", axis=1, tiled=True),
+            zone_choose(out_low),
             lax.all_gather(up_low, "dp", axis=0, tiled=True),
             lax.all_gather(down_low, "dp", axis=1, tiled=True),
             lax.all_gather(norm_low, "dp", axis=1, tiled=True),

time: 731 us -> 746 us (1.021)
  waiting for transfers between devices: 438 us -> 480 us
  blocking collectives: 128 us -> 93.9 us
    ppermute x0 -> x7, waiting for transfers between devices: none -> 32.1 us  [pair_values(): local_out = lax.ppermute(local_out, axis_name=comm_axis, perm=queue)]
    all_gather x1 -> x0, blocking collectives: 31.1 us -> none  [local(): lax.all_gather(out_low, 'dp', axis=1, tiled=True)]
    dynamic_update_slice x0 -> x8, local copies, waits for them, and re-layouts: none -> 8.71 us  [pair_values(): lax.dynamic_update_slice_in_dim(current_value, local_out, z_new * field_o...]
    unnamed x295 -> x200, local copies, waits for them, and re-layouts: 19.1 us -> 17.7 us
  transfers between devices with their start and end apart: 10 -> 17, of which waited for: 8 -> 13; matrix products, arithmetic and copies ran while one was open for 8% -> 11% of each run, Pallas kernels for 0% -> 0%
where the time goes in v1:
time: 746 us; the launch traced here: 738 us
  waiting for transfers between devices  480 us (64%)
  blocking collectives  93.9 us (13%)
  matrix products  64.2 us (9%)
  other arithmetic  44.8 us (6%)
  local copies, waits for them, and re-layouts  28.9 us (4%)
  between operations  22 us (3%)
    psum x1, waiting for transfers between devices, one_micro(): lax.psum(jnp.dot(context, out_mat, preferred_element_type=jnp.float32), '...  71.1 us
    reduce_scatter x1, waiting for transfers between devices, local(): lax.psum_scatter(grad_list[3], 'dp', scatter_dimension=1, tiled=True)  70.4 us
    reduce_scatter x1, waiting for transfers between devices, local(): lax.psum_scatter(grad_list[0], 'dp', scatter_dimension=0, tiled=True)  70.2 us
    reduce_scatter x1, waiting for transfers between devices, local(): lax.psum_scatter(grad_list[2], 'dp', scatter_dimension=0, tiled=True)  69.8 us
    psum x1, waiting for transfers between devices, one_micro(): lax.psum(jnp.einsum('tf,df->td', grad_pre, up_mat, preferred_element_type...  62 us
    psum x1, waiting for transfers between devices, one_micro(): lax.psum(jnp.dot(hidden, down_mat, preferred_element_type=jnp.float32).as...  61.1 us
    psum x1, blocking collectives, local(): grad_norm = jnp.sqrt(lax.psum(own_squares, ('dp', 'tp')))  39.6 us
    unnamed x12, waiting for transfers between devices  37.5 us
  transfers between devices with their start and end apart: 17, of which 13 were waited for; matrix products, arithmetic and copies ran while one was open for 11% of the time, Pallas kernels for 0%

profile of v1, /device:TPU:0, one launch (start us, length us, event | category | flops | bytes accessed | tf_op | source)
XLA Modules:
  0.0 738.2 jit_solution(9832678539348935529)
XLA Ops:
  15.4 19.3 %all-gather = bf16[8,96,4]{1,2,0:T(4,128)(2,1)S(1)} all-gather(bf16[1,96,4]{1,2,0:T(4,128)(2,1)S(1)} %convert_bitcast_fusion.2), channel_id=1, replica_groups=mesh['dp'=8,'tp'=4] {'dp'}, dimensions={0}, use_global_device_ids=true | all-gather | bytes 6912 | tf_op jit(solution)/shard_map/all_gather | solution.py:216
  35.6 35.0 %all_gather.17 = bf16[768,3,192]{2,1,0:T(4,128)(2,1)S(1)} all-gather(bf16[96,3,192]{2,1,0:T(4,128)(2,1)S(1)} %copy.81), channel_id=1, replica_groups=mesh['dp'=8,'tp'=4] {'dp'}, dimensions={0}, use_global_device_ids=true | all-gather | bytes 995328 | tf_op jit(solution)/shard_map/all_gather | solution.py:212
  80.0 6.4 collective-permute-done.1
  86.5 6.7 collective-permute-done.2
  93.4 6.6 collective-permute-done.3
  100.8 5.9 collective-permute-done.4
  107.2 6.5 collective-permute-done.5
  132.0 71.1 %all-reduce.9.cloned.1.call-done = (f32[512,768]{1,0:T(8,128)}, f32[512,768]{1,0:T(8,128)}) async-done(((f32[512,768]{1,0:T(8,128)}, f32[512,768]{1,0:T(8,128)}), (f32[512,768]{1,0:T(8,128)}, f32[512,768]{1,0:T(8,128)})) %all-reduce.9.cloned.1.call-update) | async-done | bytes 3145744 | tf_op jit(solution)/shard_map/psum | solution.py:104
  203.1 3.0 fusion.123
  207.8 7.5 %multiply_convert_fusion.3 = (bf16[512,768]{1,0:T(8,128)(2,1)}, f32[512,768]{1,0:T(8,128)}, f32[512,768]{1,0:T(8,128)}) fusion(bf16[768,768]{1,0:T(8,128)(2,1)} %all-gather.4.cloned.1.call-done, f32[512,768]{1,0:T(8,128)} %copy-done.9, f32[768]{0:T(1024)S(1)} %copy-done.86, f32[768]{0:T(1024)S(1)} %get-tuple-element.38, f32[512]{0:T(512)S(1)} %fusion.99, ...), kind=kOutput, calls=%fused_computation.98 | convolution fusion | flops 631504896 | bytes 6694912 | tf_op jit(solution)/shard_map/dot_general | solution.py:108
  215.4 5.5 all-gather.6.cloned.1.call-done
  220.9 3.6 add_convert_fusion.1
  227.4 5.0 multiply_convert_fusion.2
  236.7 3.3 convolution_convert_fusion.1
  241.7 62.0 %all-reduce.7.cloned.1.call-done = (f32[512,768]{1,0:T(8,128)}, f32[512,768]{1,0:T(8,128)}) async-done(((f32[512,768]{1,0:T(8,128)}, f32[512,768]{1,0:T(8,128)}), (f32[512,768]{1,0:T(8,128)}, f32[512,768]{1,0:T(8,128)})) %all-reduce.7.cloned.1.call-update) | async-done | bytes 3145744 | tf_op jit(solution)/shard_map/psum | solution.py:119
  303.7 3.8 multiply_reduce_fusion.3
  326.8 3.5 fusion.112
  333.6 61.1 %all-reduce.11.cloned.1.call-done = (bf16[512,768]{1,0:T(8,128)(2,1)}, bf16[512,768]{1,0:T(8,128)(2,1)}, bf16[512,768]{1,0:T(8,128)(2,1)}, bf16[512,768]{1,0:T(8,128)(2,1)}) async-done(((bf16[512,768]{1,0:T(8,128)(2,1)}, bf16[512,768]{1,0:T(8,128)(2,1)}, bf16[512,768]{1,0:T(8,128)(2,1)}, bf16[512,768]{1,0:T(8,128)(2,1)}), (bf16[512,768]{1,0:T(8,128)(2,1)}, bf16[512,768]{1,0:T(8,128)(2,1)}, ...) | async-done | bytes 3145744 | tf_op jit(solution)/shard_map/psum | solution.py:111
  400.5 4.3 convolution_add_fusion.1
  424.9 37.3 %reduce-scatter.18.cloned.1.call-done = f32[96,4]{1,0:T(8,128)} async-done(((f32[768,4]{1,0:T(8,128)}), f32[96,4]{1,0:T(8,128)}) %reduce-scatter.18.cloned.1.call-update) | async-done | bytes 1552
  464.3 69.8 %reduce-scatter.12.cloned.1.call-done = f32[96,768]{1,0:T(8,128)} async-done(((f32[768,768]{1,0:T(8,128)}), f32[96,768]{1,0:T(8,128)}) %reduce-scatter.12.cloned.1.call-update) | async-done | bytes 294928 | tf_op jit(solution)/shard_map/reduce_scatter | solution.py:224
  535.7 70.4 %reduce-scatter.14.cloned.1.call-done = f32[768,96]{0,1:T(8,128)} async-done(((f32[768,768]{0,1:T(8,128)}), f32[768,96]{0,1:T(8,128)}) %reduce-scatter.14.cloned.1.call-update) | async-done | bytes 294928 | tf_op jit(solution)/shard_map/reduce_scatter | solution.py:225
  607.8 70.2 %reduce-scatter.10.cloned.1.call-done = f32[96,3,192]{2,0,1:T(8,128)} async-done(((f32[768,3,192]{2,0,1:T(8,128)}), f32[96,3,192]{2,0,1:T(8,128)}) %reduce-scatter.10.cloned.1.call-update) | async-done | bytes 221200 | tf_op jit(solution)/shard_map/reduce_scatter | solution.py:222
  683.7 39.6 %psum.71 = f32[]{:T(128)} all-reduce(f32[]{:T(128)S(6)} %add.411), channel_id=1, replica_groups=mesh['dp'=8,'tp'=4] {'dp','tp'}, use_global_device_ids=true, to_apply=%region_53.54 | all-reduce | flops 1 | bytes 8 | tf_op jit(solution)/shard_map/psum | solution.py:240
  (345 shorter events, 108.6 us)
Async XLA Ops:
  8.0 195.1 %all-reduce.9.cloned.1.call-start = ((), (), s32[]{:S(2)}) async-start(), calls=%async_computation.13 | async-start | bytes 6291456 | tf_op jit(solution)/shard_map/psum | solution.py:104
  9.1 70.4 %collective-permute-start = (bf16[192,96]{1,0:T(8,128)(2,1)S(1)}, bf16[192,96]{1,0:T(8,128)(2,1)S(1)}, u32[]{:S(2)}, u32[]{:S(2)}) collective-permute-start(bf16[192,96]{1,0:T(8,128)(2,1)S(1)} %convert_element_type.170), channel_id=1, source_target_pairs={{0,4},{4,8},{8,12},{12,16},{16,20},{20,24},{24,28},{28,0},{1,5},{5... | collective-permute-start | bytes 110600 | tf_op jit(solution)/shard_map/ppermute | solution.py:38
  15.4 57.4 %copy-start.82 = (f32[512]{0:T(512)}, f32[512]{0:T(512)S(1)}, u32[]{:S(2)}) copy-start(f32[512]{0:T(512)S(1)} %get-tuple-element.32) | copy-start | bytes 6148
  15.4 60.3 %copy-start.84 = (f32[512]{0:T(512)}, f32[512]{0:T(512)S(1)}, u32[]{:S(2)}) copy-start(f32[512]{0:T(512)S(1)} %get-tuple-element.33) | copy-start | bytes 6148
  79.5 6.8 collective-permute-start.1
  86.4 6.8 collective-permute-start.2
  93.2 6.8 collective-permute-start.3
  100.0 6.8 collective-permute-start.4
  106.8 6.9 collective-permute-start.5
  113.6 9.4 %collective-permute-start.6 = (bf16[192,96]{1,0:T(8,128)(2,1)}, bf16[192,96]{1,0:T(8,128)(2,1)}, u32[]{:S(2)}, u32[]{:S(2)}) collective-permute-start(bf16[192,96]{1,0:T(8,128)(2,1)} %collective-permute-done.5), channel_id=1, source_target_pairs={{0,4},{4,8},{8,12},{12,16},{16,20},{20,24},{24,28},{28,0},{1,5},{5... | collective-permute-start | bytes 110600 | tf_op jit(solution)/shard_map/ppermute | solution.py:38
  128.5 79.3 %all-gather.4.cloned.1.call-start = ((), (), s32[]{:S(2)}) async-start(), calls=%async_computation.5 | async-start | bytes 1327104 | tf_op jit(solution)/shard_map/all_gather | solution.py:214
  130.3 90.6 %all-gather.6.cloned.1.call-start = ((), (), s32[]{:S(2)}) async-start(), calls=%async_computation.6 | async-start | bytes 1327104 | tf_op jit(solution)/shard_map/all_gather | solution.py:215
  132.0 171.7 %all-reduce.7.cloned.1.call-start = ((), (), s32[]{:S(2)}) async-start(), calls=%async_computation.12 | async-start | bytes 6291456 | tf_op jit(solution)/shard_map/psum | solution.py:119
  236.4 158.4 %all-reduce.11.cloned.1.call-start = ((), (), s32[]{:S(2)}) async-start(), calls=%async_computation.14 | async-start | bytes 6291456 | tf_op jit(solution)/shard_map/psum | solution.py:111
  325.5 89.8 %reduce-scatter.16.cloned.1.call-start = ((), (), s32[]{:S(2)}) async-start(), calls=%async_computation.10 | async-start | bytes 884736
  332.1 62.6 %copy-start.4 = (bf16[2,512,768]{2,1,0:T(8,128)(2,1)S(1)}, bf16[2,512,768]{2,1,0:T(8,128)(2,1)}, u32[]{:S(2)}) copy-start(bf16[2,512,768]{2,1,0:T(8,128)(2,1)} %param.19) | copy-start | bytes 4718596
  333.3 128.8 %reduce-scatter.18.cloned.1.call-start = ((), (), s32[]{:S(2)}) async-start(), calls=%async_computation.11 | async-start | bytes 442368
  400.4 133.7 %reduce-scatter.12.cloned.1.call-start = ((), (), s32[]{:S(2)}) async-start(), calls=%async_computation.8 | async-start | bytes 2654208 | tf_op jit(solution)/shard_map/reduce_scatter | solution.py:224
  404.9 201.3 %reduce-scatter.14.cloned.1.call-start = ((), (), s32[]{:S(2)}) async-start(), calls=%async_computation.9 | async-start | bytes 2654208 | tf_op jit(solution)/shard_map/reduce_scatter | solution.py:225
  409.6 268.4 %reduce-scatter.10.cloned.1.call-start = ((), (), s32[]{:S(2)}) async-start(), calls=%async_computation.7 | async-start | bytes 2654208 | tf_op jit(solution)/shard_map/reduce_scatter | solution.py:222
  424.7 257.6 %copy-start.29 = (bf16[1,512,768]{2,1,0:T(8,128)(2,1)S(1)}, bf16[1,512,768]{2,1,0:T(8,128)(2,1)}, u32[]{:S(2)}) copy-start(bf16[1,512,768]{2,1,0:T(8,128)(2,1)} %fusion.68) | copy-start | bytes 2359300
  683.7 43.9 %copy-start.42 = (f32[96,768]{1,0:T(8,128)S(1)}, f32[96,768]{1,0:T(8,128)}, u32[]{:S(2)}) copy-start(f32[96,768]{1,0:T(8,128)} %reduce-scatter.12.cloned.1.call-done) | copy-start | bytes 884740
  683.7 43.9 %copy-start.61 = (f32[96,768]{1,0:T(8,128)S(1)}, f32[96,768]{1,0:T(8,128)}, u32[]{:S(2)}) copy-start(f32[96,768]{1,0:T(8,128)} %param.30) | copy-start | bytes 884740
  683.7 43.9 %copy-start.62 = (f32[96,768]{1,0:T(8,128)S(1)}, f32[96,768]{1,0:T(8,128)}, u32[]{:S(2)}) copy-start(f32[96,768]{1,0:T(8,128)} %param.35) | copy-start | bytes 884740
  (91 other events, 786.7 us)
Sparse Core Ops, SparseCore 0:
  128.7 74.3 all-reduce.8
  236.5 67.1 all-reduce.6
  325.6 69.1 all-reduce.10
Sparse Core Ops, SparseCore 1:
  131.8 47.0 all-gather.3
  180.9 39.9 all-gather.5
  333.4 62.4 reduce-scatter.15
  400.5 61.6 reduce-scatter.17
  466.1 68.0 reduce-scatter.11
  538.0 68.1 reduce-scatter.13
  609.9 68.0 reduce-scatter.9
